TPU v7x, 256 devices: a whole 4x4x8 slice. The times are simulated.
256 devices in a mesh: row: 16 (over z_hi, y), col: 16 (over x, z_lo, core).
Axes of the slice: x: 4, y: 4, z: 8 (z_hi: 4, z_lo: 2; z = z_hi * 2 + z_lo), core: 2. Of those that a mesh axis runs over, the one named last changes fastest.
Arguments:
- positions: float32 [3, 32768], P(None, ('row', 'col')), may hold values from 0 to 1
- radii: float32 [32768], P(('row', 'col')), may hold values from 0.5 to 2
- right_side: float32 [32768, 256], P(('row', 'col')), may hold values from -60 to 60, as said below
Outputs:
- solution: float32 [32768, 256], P(('row', 'col'))
- residual: float32 [32768, 256], P(('row', 'col'))
Inputs may be any that keep to these rules, and one draw needn't show every extreme that they name: `right_side`: real values of varying scale.
All inputs are finite; a program needn't handle non-finite values.
Results may differ from a plain program's by a relative error of at most 0.0003.
Values sent between devices are 32-bit elements; how exact they have to be, the bound alone decides.
A program may use at most 64 MiB of HBM per device.

v0:
```python
import jax
import jax.numpy as jnp
from jax import lax
from jax.sharding import PartitionSpec as P

ITERS = 2


def kernel_product(row_points, col_points, values, kernel_scale, softening, limit):
    row_count = row_points.shape[1]
    col_count = col_points.shape[1]
    blocks = max(1, row_count * col_count // limit)
    while row_count % blocks:
        blocks = blocks - 1
    block_size = row_count // blocks
    grouped = row_points.reshape(3, blocks, block_size).transpose(1, 0, 2)

    def apply_block(row_block):
        first = row_block[0][:, None] - col_points[0][None, :]
        second = row_block[1][:, None] - col_points[1][None, :]
        third = row_block[2][:, None] - col_points[2][None, :]
        squared = first * first + second * second + third * third
        weights = lax.rsqrt(squared + softening) * kernel_scale
        return jnp.dot(
            weights, values, preferred_element_type=jnp.float32, precision=lax.Precision.HIGHEST
        )

    return lax.map(apply_block, grouped).reshape(row_count, values.shape[1])


def constants(total):
    kernel_scale = float(total) ** (-0.5)
    spacing = 0.25 * float(total) ** (-1.0 / 3.0)
    return (kernel_scale, spacing * spacing)


def squares(residual):
    return lax.psum(jnp.sum(residual * residual, axis=0), ("row", "col"))


def body(positions, radii, right_side):
    local_count = positions.shape[1]
    total = local_count * lax.axis_size("row") * lax.axis_size("col")
    kernel_scale, softening = constants(total)
    row_points = lax.all_gather(positions, "col", axis=1, tiled=True)
    col_points = lax.all_gather(positions, "row", axis=1, tiled=True)
    limit = 1 << 20
    solution = jnp.zeros_like(right_side)
    residual = right_side
    direction = right_side
    norm_now = squares(residual)
    for iteration in range(ITERS):
        col_values = lax.all_gather(direction, "row", axis=0, tiled=True)
        summed = lax.psum_scatter(
            kernel_product(row_points, col_points, col_values, kernel_scale, softening, limit),
            "col",
            scatter_dimension=0,
            tiled=True,
        )
        image_vec = direction / radii[:, None] + summed
        curvature = lax.psum(jnp.sum(direction * image_vec, axis=0), ("row", "col"))
        step_size = norm_now / curvature
        solution = solution + step_size * direction
        residual = residual - step_size * image_vec
        if iteration + 1 < ITERS:
            norm_next = squares(residual)
            direction = residual + norm_next / norm_now * direction
            norm_now = norm_next
    return (solution, residual)


def solution(mesh):
    return jax.shard_map(
        body,
        mesh=mesh,
        in_specs=(P(None, ("row", "col")), P(("row", "col")), P(("row", "col"), None)),
        out_specs=(P(("row", "col"), None), P(("row", "col"), None)),
        check_vma=False,
    )
```

profile of v0, /device:TPU:1, one launch (start us, length us, event | category | flops | bytes accessed | tf_op | source)
XLA Modules:
  0.0 550.6 jit_solution(2993443880854321543)
XLA Ops:
  7.9 40.7 %all_gather.13 = f32[3,2048]{1,0:T(4,128)S(1)} all-gather(f32[3,128]{1,0:T(4,128)} %param.7), channel_id=1, replica_groups=mesh['row'=16,'col'=16] {'row'}, dimensions={1}, use_global_device_ids=true | all-gather | bytes 26112 | tf_op jit(solution)/shard_map/all_gather | solution.py:46
  48.7 28.0 %all_gather.12 = f32[3,2048]{1,0:T(4,128)S(1)} all-gather(f32[3,128]{1,0:T(4,128)} %param.7), channel_id=1, replica_groups=mesh['row'=16,'col'=16] {'col'}, dimensions={1}, use_global_device_ids=true | all-gather | bytes 26112 | tf_op jit(solution)/shard_map/all_gather | solution.py:45
  76.8 25.9 %while.20 = (s32[]{:T(128)}, f32[4,512,256]{2,1,0:T(8,128)S(1)}, f32[4,3,512]{2,1,0:T(4,128)S(1)}, f32[3,2048]{1,0:T(4,128)S(1)}, f32[2048,256]{1,0:T(8,128)}, /*index=5*/s32[]{:T(128)}, s32[]{:T(128)}, s32[]{}, s32[]{}) while((s32[]{:T(128)}, f32[4,512,256]{2,1,0:T(8,128)S(1)}, f32[4,3,512]{2,1,0:T(4,128)S(1)}, f32[3,2048]{1,0:T(4,128)S(1)}, ...), condition=%wide.region_3.4_spmd, body=%wide.region_2.3_spmd.sunk | while | flops 3231711232 | bytes 2713733 | solution.py:28
  76.8 6.4 %fusion.71 = f32[4,512,256]{2,1,0:T(8,128)S(1)} fusion(f32[4,512,256]{2,1,0:T(8,128)S(1)} %get-tuple-element.194, s32[]{:T(128)} %get-tuple-element.193, f32[2048,256]{1,0:T(8,128)} %get-tuple-element.206, f32[2048]{0:T(1024)S(1)} %bitcast.63, f32[512]{0:T(512)S(1)} %bitcast.70, f32[2048]{0:T(1024)S(1)} %bitcast.64, f32[512]{0:T(512)S(1)} %bitcast.69, ...), kind=kOutput, calls=%fused_computation.21.clone.1 | convolution fusion | flops 3231711232 | bytes 2652164 | tf_op jit(solution)/shard_map/while/body/eval_jaxpr/dot_general | solution.py:24
  83.3 6.4 %fusion.71 = f32[4,512,256]{2,1,0:T(8,128)S(1)} fusion(f32[4,512,256]{2,1,0:T(8,128)S(1)} %get-tuple-element.194, s32[]{:T(128)} %get-tuple-element.193, f32[2048,256]{1,0:T(8,128)} %get-tuple-element.206, f32[2048]{0:T(1024)S(1)} %bitcast.63, f32[512]{0:T(512)S(1)} %bitcast.70, f32[2048]{0:T(1024)S(1)} %bitcast.64, f32[512]{0:T(512)S(1)} %bitcast.69, ...), kind=kOutput, calls=%fused_computation.21.clone.1 | convolution fusion | flops 3231711232 | bytes 2652164 | tf_op jit(solution)/shard_map/while/body/eval_jaxpr/dot_general | solution.py:24
  89.8 6.4 %fusion.71 = f32[4,512,256]{2,1,0:T(8,128)S(1)} fusion(f32[4,512,256]{2,1,0:T(8,128)S(1)} %get-tuple-element.194, s32[]{:T(128)} %get-tuple-element.193, f32[2048,256]{1,0:T(8,128)} %get-tuple-element.206, f32[2048]{0:T(1024)S(1)} %bitcast.63, f32[512]{0:T(512)S(1)} %bitcast.70, f32[2048]{0:T(1024)S(1)} %bitcast.64, f32[512]{0:T(512)S(1)} %bitcast.69, ...), kind=kOutput, calls=%fused_computation.21.clone.1 | convolution fusion | flops 3231711232 | bytes 2652164 | tf_op jit(solution)/shard_map/while/body/eval_jaxpr/dot_general | solution.py:24
  96.3 6.4 %fusion.71 = f32[4,512,256]{2,1,0:T(8,128)S(1)} fusion(f32[4,512,256]{2,1,0:T(8,128)S(1)} %get-tuple-element.194, s32[]{:T(128)} %get-tuple-element.193, f32[2048,256]{1,0:T(8,128)} %get-tuple-element.206, f32[2048]{0:T(1024)S(1)} %bitcast.63, f32[512]{0:T(512)S(1)} %bitcast.70, f32[2048]{0:T(1024)S(1)} %bitcast.64, f32[512]{0:T(512)S(1)} %bitcast.69, ...), kind=kOutput, calls=%fused_computation.21.clone.1 | convolution fusion | flops 3231711232 | bytes 2652164 | tf_op jit(solution)/shard_map/while/body/eval_jaxpr/dot_general | solution.py:24
  102.7 1.3 copy-done.1
  104.1 58.5 %reduce-scatter.3.cloned.1.call-done = f32[128,256]{1,0:T(8,128)} async-done(((f32[2048,256]{1,0:T(8,128)}), f32[128,256]{1,0:T(8,128)}) %reduce-scatter.3.cloned.1.call-update) | async-done | bytes 131088 | tf_op jit(solution)/shard_map/reduce_scatter | solution.py:54
  162.6 1.0 multiply_reduce_fusion.2
  163.6 79.5 %all-reduce = (f32[256]{0:T(256)S(1)}, f32[256]{0:T(256)S(1)}) all-reduce(f32[256]{0:T(256)S(1)} %get-tuple-element.59, f32[256]{0:T(256)S(1)} %get-tuple-element.58), channel_id=1, replica_groups=mesh['row'=16,'col'=16] {'row','col'}, use_global_device_ids=true, to_apply=%region_1.0 | all-reduce | flops 512 | bytes 4096 | tf_op jit(solution)/shard_map/psum | solution.py:38
  243.1 1.0 multiply_reduce_fusion.1
  244.1 72.5 %psum.30 = f32[256]{0:T(256)S(1)} all-reduce(f32[256]{0:T(256)S(1)} %get-tuple-element.82), channel_id=1, replica_groups=mesh['row'=16,'col'=16] {'row','col'}, use_global_device_ids=true, to_apply=%region_8.9 | all-reduce | flops 256 | bytes 2048 | tf_op jit(solution)/shard_map/psum | solution.py:38
  317.6 55.1 %all-gather.5.cloned.1.call-done = f32[2048,256]{1,0:T(8,128)} async-done(((f32[128,256]{1,0:T(8,128)}), f32[2048,256]{1,0:T(8,128)}) %all-gather.5.cloned.1.call-update) | async-done | bytes 2097168 | tf_op jit(solution)/shard_map/all_gather | solution.py:53
  372.9 25.9 %while.21 = (s32[]{:T(128)}, f32[4,512,256]{2,1,0:T(8,128)S(1)}, f32[4,3,512]{2,1,0:T(4,128)S(1)}, f32[3,2048]{1,0:T(4,128)S(1)}, f32[2048,256]{1,0:T(8,128)}, /*index=5*/s32[]{:T(128)}, s32[]{:T(128)}, s32[]{}, s32[]{}) while((s32[]{:T(128)}, f32[4,512,256]{2,1,0:T(8,128)S(1)}, f32[4,3,512]{2,1,0:T(4,128)S(1)}, f32[3,2048]{1,0:T(4,128)S(1)}, ...), condition=%wide.region_10.11_spmd, body=%wide.region_9.10_spmd.sunk | while | flops 3231711232 | bytes 2713733 | solution.py:28
  372.9 6.4 %fusion.75 = f32[4,512,256]{2,1,0:T(8,128)S(1)} fusion(f32[4,512,256]{2,1,0:T(8,128)S(1)} %get-tuple-element.221, s32[]{:T(128)} %get-tuple-element.220, f32[2048,256]{1,0:T(8,128)} %get-tuple-element.233, f32[2048]{0:T(1024)S(1)} %bitcast.66, f32[512]{0:T(512)S(1)} %bitcast.73, f32[2048]{0:T(1024)S(1)} %bitcast.67, f32[512]{0:T(512)S(1)} %bitcast.72, ...), kind=kOutput, calls=%fused_computation.48.clone.1 | convolution fusion | flops 3231711232 | bytes 2652164 | tf_op jit(solution)/shard_map/while/body/eval_jaxpr/dot_general | solution.py:24
  379.4 6.4 %fusion.75 = f32[4,512,256]{2,1,0:T(8,128)S(1)} fusion(f32[4,512,256]{2,1,0:T(8,128)S(1)} %get-tuple-element.221, s32[]{:T(128)} %get-tuple-element.220, f32[2048,256]{1,0:T(8,128)} %get-tuple-element.233, f32[2048]{0:T(1024)S(1)} %bitcast.66, f32[512]{0:T(512)S(1)} %bitcast.73, f32[2048]{0:T(1024)S(1)} %bitcast.67, f32[512]{0:T(512)S(1)} %bitcast.72, ...), kind=kOutput, calls=%fused_computation.48.clone.1 | convolution fusion | flops 3231711232 | bytes 2652164 | tf_op jit(solution)/shard_map/while/body/eval_jaxpr/dot_general | solution.py:24
  385.9 6.4 %fusion.75 = f32[4,512,256]{2,1,0:T(8,128)S(1)} fusion(f32[4,512,256]{2,1,0:T(8,128)S(1)} %get-tuple-element.221, s32[]{:T(128)} %get-tuple-element.220, f32[2048,256]{1,0:T(8,128)} %get-tuple-element.233, f32[2048]{0:T(1024)S(1)} %bitcast.66, f32[512]{0:T(512)S(1)} %bitcast.73, f32[2048]{0:T(1024)S(1)} %bitcast.67, f32[512]{0:T(512)S(1)} %bitcast.72, ...), kind=kOutput, calls=%fused_computation.48.clone.1 | convolution fusion | flops 3231711232 | bytes 2652164 | tf_op jit(solution)/shard_map/while/body/eval_jaxpr/dot_general | solution.py:24
  392.3 6.4 %fusion.75 = f32[4,512,256]{2,1,0:T(8,128)S(1)} fusion(f32[4,512,256]{2,1,0:T(8,128)S(1)} %get-tuple-element.221, s32[]{:T(128)} %get-tuple-element.220, f32[2048,256]{1,0:T(8,128)} %get-tuple-element.233, f32[2048]{0:T(1024)S(1)} %bitcast.66, f32[512]{0:T(512)S(1)} %bitcast.73, f32[2048]{0:T(1024)S(1)} %bitcast.67, f32[512]{0:T(512)S(1)} %bitcast.72, ...), kind=kOutput, calls=%fused_computation.48.clone.1 | convolution fusion | flops 3231711232 | bytes 2652164 | tf_op jit(solution)/shard_map/while/body/eval_jaxpr/dot_general | solution.py:24
  398.8 1.3 copy-done
  400.1 61.9 %reduce-scatter.5.cloned.1.call-done = f32[128,256]{1,0:T(8,128)} async-done(((f32[2048,256]{1,0:T(8,128)}), f32[128,256]{1,0:T(8,128)}) %reduce-scatter.5.cloned.1.call-update) | async-done | bytes 131088 | tf_op jit(solution)/shard_map/reduce_scatter | solution.py:54
  462.0 1.0 multiply_reduce_fusion
  463.0 79.4 %psum.31 = f32[256]{0:T(256)S(1)} all-reduce(f32[256]{0:T(256)S(1)} %multiply_reduce_fusion), channel_id=1, replica_groups=mesh['row'=16,'col'=16] {'row','col'}, use_global_device_ids=true, to_apply=%region_13.14 | all-reduce | flops 256 | bytes 2048 | tf_op jit(solution)/shard_map/psum | solution.py:61
  542.4 1.7 multiply_subtract_fusion
  (39 shorter events, 2.4 us)
Async XLA Ops:
  7.2 69.5 %all-gather.3.cloned.1.call-start = ((), (), s32[]{:S(2)}) async-start(), calls=%async_computation.2 | async-start | bytes 2228224 | tf_op jit(solution)/shard_map/all_gather | solution.py:53
  7.9 154.7 %reduce-scatter.3.cloned.1.call-start = ((), (), s32[]{:S(2)}) async-start(), calls=%async_computation.3 | async-start | bytes 2228224 | tf_op jit(solution)/shard_map/reduce_scatter | solution.py:54
  102.7 1.3 copy-start.1
  102.7 59.9 %copy-start.2 = (f32[128,256]{1,0:T(8,128)S(1)}, f32[128,256]{1,0:T(8,128)}, u32[]{:S(2)}) copy-start(f32[128,256]{1,0:T(8,128)} %param.9) | copy-start | bytes 393220
  102.7 59.9 %copy-start.4 = (f32[128]{0:T(128)S(1)}, f32[128]{0:T(128)}, u32[]{:S(2)}) copy-start(f32[128]{0:T(128)} %param.8) | copy-start | bytes 1540
  104.1 268.6 %all-gather.5.cloned.1.call-start = ((), (), s32[]{:S(2)}) async-start(), calls=%async_computation.4 | async-start | bytes 2228224 | tf_op jit(solution)/shard_map/all_gather | solution.py:53
  317.3 144.7 %reduce-scatter.5.cloned.1.call-start = ((), (), s32[]{:S(2)}) async-start(), calls=%async_computation.5 | async-start | bytes 2228224 | tf_op jit(solution)/shard_map/reduce_scatter | solution.py:54
  398.7 1.3 copy-start
  398.7 63.2 %copy-start.3 = (f32[128,256]{1,0:T(8,128)S(1)}, f32[128,256]{1,0:T(8,128)}, u32[]{:S(2)}) copy-start(f32[128,256]{1,0:T(8,128)} %multiply_add_fusion.1) | copy-start | bytes 393220
Sparse Core Ops, SparseCore 0:
  10.4 62.6 all-gather.2
  104.2 58.3 reduce-scatter.2
  317.4 55.2 all-gather.4
  400.2 61.7 reduce-scatter.4
where the time goes:
time: 551 us
  blocking collectives  300 us (54%)
  waiting for transfers between devices  176 us (32%)
  matrix products  51.2 us (9%)
  between operations  13.8 us (3%)
    psum x2, blocking collectives, squares(): return lax.psum(jnp.sum(residual * residual, axis=0), ('row', 'col'))  152 us
    reduce_scatter x2, waiting for transfers between devices, body(): lax.psum_scatter(kernel_product(row_points, col_points, col_values, kerne...  120 us
    psum x1, blocking collectives, body(): curvature = lax.psum(jnp.sum(direction * image_vec, axis=0), ('row', 'col'))  79.4 us
    all_gather x2, waiting for transfers between devices, body(): col_values = lax.all_gather(direction, 'row', axis=0, tiled=True)  55.1 us
    dot_general x8, matrix products, apply_block(): jnp.dot(weights, values, preferred_element_type=jnp.float32, precision=la...  51.2 us
    all_gather x1, blocking collectives, body(): col_points = lax.all_gather(positions, 'row', axis=1, tiled=True)  40.7 us
    all_gather x1, blocking collectives, body(): row_points = lax.all_gather(positions, 'col', axis=1, tiled=True)  28 us
  transfers between devices with their start and end apart: 4, of which 3 were waited for; matrix products, arithmetic and copies ran while one was open for 0% of the time, Pallas kernels for 0%

commit v1 on v0

--- a/solution.py
+++ b/solution.py
@@ -4,6 +4,11 @@
 from jax.sharding import PartitionSpec as P
 
 ITERS = 2
+
+
+def one_after_other(value, leading, second_2):
+    inner = lax.psum(value, leading)
+    return lax.psum(inner, second_2)
 
 
 def kernel_product(row_points, col_points, values, kernel_scale, softening, limit):
@@ -35,7 +40,7 @@
 
 
 def squares(residual):
-    return lax.psum(jnp.sum(residual * residual, axis=0), ("row", "col"))
+    return one_after_other(jnp.sum(residual * residual, axis=0), "col", "row")
 
 
 def body(positions, radii, right_side):

time: 551 us -> 615 us (1.12)
  blocking collectives: 300 us -> 358 us
    psum x1 -> x2, blocking collectives: 79.4 us -> 159 us  [body(): curvature = lax.psum(jnp.sum(direction * image_vec, axis=0), ('row', 'col'))]
    psum x2 -> x4, blocking collectives: 152 us -> 130 us  [the longest x2 71.8 us: one_after_other(): return lax.psum(inner, second_2)]
where the time goes in v1:
time: 615 us
  blocking collectives  358 us (58%)
  waiting for transfers between devices  182 us (30%)
  matrix products  51.2 us (8%)
  between operations  13.8 us (2%)
    psum x2, blocking collectives, body(): curvature = lax.psum(jnp.sum(direction * image_vec, axis=0), ('row', 'col'))  159 us
    reduce_scatter x2, waiting for transfers between devices, body(): lax.psum_scatter(kernel_product(row_points, col_points, col_values, kerne...  120 us
    psum x2, blocking collectives, one_after_other(): return lax.psum(inner, second_2)  71.8 us
    all_gather x2, waiting for transfers between devices, body(): col_values = lax.all_gather(direction, 'row', axis=0, tiled=True)  61 us
    psum x2, blocking collectives, one_after_other(): inner = lax.psum(value, leading)  58.7 us
    dot_general x8, matrix products, apply_block(): jnp.dot(weights, values, preferred_element_type=jnp.float32, precision=la...  51.2 us
    all_gather x1, blocking collectives, body(): col_points = lax.all_gather(positions, 'row', axis=1, tiled=True)  40.7 us
    all_gather x1, blocking collectives, body(): row_points = lax.all_gather(positions, 'col', axis=1, tiled=True)  28 us
  transfers between devices with their start and end apart: 4, of which 3 were waited for; matrix products, arithmetic and copies ran while one was open for 0% of the time, Pallas kernels for 0%

profile of v1, /device:TPU:1, one launch (start us, length us, event | category | flops | bytes accessed | tf_op | source)
XLA Modules:
  0.0 614.7 jit_solution(5319018064573894291)
XLA Ops:
  7.9 40.7 %all_gather.13 = f32[3,2048]{1,0:T(4,128)S(1)} all-gather(f32[3,128]{1,0:T(4,128)} %param.7), channel_id=1, replica_groups=mesh['row'=16,'col'=16] {'row'}, dimensions={1}, use_global_device_ids=true | all-gather | bytes 26112 | tf_op jit(solution)/shard_map/all_gather | solution.py:51
  48.7 28.0 %all_gather.12 = f32[3,2048]{1,0:T(4,128)S(1)} all-gather(f32[3,128]{1,0:T(4,128)} %param.7), channel_id=1, replica_groups=mesh['row'=16,'col'=16] {'col'}, dimensions={1}, use_global_device_ids=true | all-gather | bytes 26112 | tf_op jit(solution)/shard_map/all_gather | solution.py:50
  76.8 25.9 %while.20 = (s32[]{:T(128)}, f32[4,512,256]{2,1,0:T(8,128)S(1)}, f32[4,3,512]{2,1,0:T(4,128)S(1)}, f32[3,2048]{1,0:T(4,128)S(1)}, f32[2048,256]{1,0:T(8,128)}, /*index=5*/s32[]{:T(128)}, s32[]{:T(128)}, s32[]{}, s32[]{}) while((s32[]{:T(128)}, f32[4,512,256]{2,1,0:T(8,128)S(1)}, f32[4,3,512]{2,1,0:T(4,128)S(1)}, f32[3,2048]{1,0:T(4,128)S(1)}, ...), condition=%wide.region_4.5_spmd, body=%wide.region_3.4_spmd.sunk | while | flops 3231711232 | bytes 2713733 | solution.py:33
  76.8 6.4 %fusion.71 = f32[4,512,256]{2,1,0:T(8,128)S(1)} fusion(f32[4,512,256]{2,1,0:T(8,128)S(1)} %get-tuple-element.192, s32[]{:T(128)} %get-tuple-element.191, f32[2048,256]{1,0:T(8,128)} %get-tuple-element.204, f32[2048]{0:T(1024)S(1)} %bitcast.63, f32[512]{0:T(512)S(1)} %bitcast.70, f32[2048]{0:T(1024)S(1)} %bitcast.64, f32[512]{0:T(512)S(1)} %bitcast.69, ...), kind=kOutput, calls=%fused_computation.21.clone.1 | convolution fusion | flops 3231711232 | bytes 2652164 | tf_op jit(solution)/shard_map/while/body/eval_jaxpr/dot_general | solution.py:29
  83.3 6.4 %fusion.71 = f32[4,512,256]{2,1,0:T(8,128)S(1)} fusion(f32[4,512,256]{2,1,0:T(8,128)S(1)} %get-tuple-element.192, s32[]{:T(128)} %get-tuple-element.191, f32[2048,256]{1,0:T(8,128)} %get-tuple-element.204, f32[2048]{0:T(1024)S(1)} %bitcast.63, f32[512]{0:T(512)S(1)} %bitcast.70, f32[2048]{0:T(1024)S(1)} %bitcast.64, f32[512]{0:T(512)S(1)} %bitcast.69, ...), kind=kOutput, calls=%fused_computation.21.clone.1 | convolution fusion | flops 3231711232 | bytes 2652164 | tf_op jit(solution)/shard_map/while/body/eval_jaxpr/dot_general | solution.py:29
  89.8 6.4 %fusion.71 = f32[4,512,256]{2,1,0:T(8,128)S(1)} fusion(f32[4,512,256]{2,1,0:T(8,128)S(1)} %get-tuple-element.192, s32[]{:T(128)} %get-tuple-element.191, f32[2048,256]{1,0:T(8,128)} %get-tuple-element.204, f32[2048]{0:T(1024)S(1)} %bitcast.63, f32[512]{0:T(512)S(1)} %bitcast.70, f32[2048]{0:T(1024)S(1)} %bitcast.64, f32[512]{0:T(512)S(1)} %bitcast.69, ...), kind=kOutput, calls=%fused_computation.21.clone.1 | convolution fusion | flops 3231711232 | bytes 2652164 | tf_op jit(solution)/shard_map/while/body/eval_jaxpr/dot_general | solution.py:29
  96.3 6.4 %fusion.71 = f32[4,512,256]{2,1,0:T(8,128)S(1)} fusion(f32[4,512,256]{2,1,0:T(8,128)S(1)} %get-tuple-element.192, s32[]{:T(128)} %get-tuple-element.191, f32[2048,256]{1,0:T(8,128)} %get-tuple-element.204, f32[2048]{0:T(1024)S(1)} %bitcast.63, f32[512]{0:T(512)S(1)} %bitcast.70, f32[2048]{0:T(1024)S(1)} %bitcast.64, f32[512]{0:T(512)S(1)} %bitcast.69, ...), kind=kOutput, calls=%fused_computation.21.clone.1 | convolution fusion | flops 3231711232 | bytes 2652164 | tf_op jit(solution)/shard_map/while/body/eval_jaxpr/dot_general | solution.py:29
  102.7 1.3 copy-done.1
  104.1 58.5 %reduce-scatter.3.cloned.1.call-done = f32[128,256]{1,0:T(8,128)} async-done(((f32[2048,256]{1,0:T(8,128)}), f32[128,256]{1,0:T(8,128)}) %reduce-scatter.3.cloned.1.call-update) | async-done | bytes 131088 | tf_op jit(solution)/shard_map/reduce_scatter | solution.py:59
  163.6 30.9 %psum.42 = f32[256]{0:T(256)S(1)} all-reduce(f32[256]{0:T(256)S(1)} %get-tuple-element.59), channel_id=1, replica_groups=mesh['row'=16,'col'=16] {'col'}, use_global_device_ids=true, to_apply=%region_1.0 | all-reduce | flops 256 | bytes 2048 | tf_op jit(solution)/shard_map/psum | solution.py:10
  194.5 37.1 %psum.43 = f32[256]{0:T(256)S(1)} all-reduce(f32[256]{0:T(256)S(1)} %psum.42), channel_id=1, replica_groups=mesh['row'=16,'col'=16] {'row'}, use_global_device_ids=true, to_apply=%region_2.0 | all-reduce | flops 256 | bytes 2048 | tf_op jit(solution)/shard_map/psum | solution.py:11
  231.6 79.6 %psum.44 = f32[256]{0:T(256)S(1)} all-reduce(f32[256]{0:T(256)S(1)} %get-tuple-element.58), channel_id=1, replica_groups=mesh['row'=16,'col'=16] {'row','col'}, use_global_device_ids=true, to_apply=%region_7.8 | all-reduce | flops 256 | bytes 2048 | tf_op jit(solution)/shard_map/psum | solution.py:66
  312.3 27.8 %psum.45 = f32[256]{0:T(256)S(1)} all-reduce(f32[256]{0:T(256)S(1)} %get-tuple-element.80), channel_id=1, replica_groups=mesh['row'=16,'col'=16] {'col'}, use_global_device_ids=true, to_apply=%region_9.10 | all-reduce | flops 256 | bytes 2048 | tf_op jit(solution)/shard_map/psum | solution.py:10
  340.1 34.7 %psum.46 = f32[256]{0:T(256)S(1)} all-reduce(f32[256]{0:T(256)S(1)} %psum.45), channel_id=1, replica_groups=mesh['row'=16,'col'=16] {'row'}, use_global_device_ids=true, to_apply=%region_10.11 | all-reduce | flops 256 | bytes 2048 | tf_op jit(solution)/shard_map/psum | solution.py:11
  375.7 61.0 %all-gather.5.cloned.1.call-done = f32[2048,256]{1,0:T(8,128)} async-done(((f32[128,256]{1,0:T(8,128)}), f32[2048,256]{1,0:T(8,128)}) %all-gather.5.cloned.1.call-update) | async-done | bytes 2097168 | tf_op jit(solution)/shard_map/all_gather | solution.py:58
  436.9 25.9 %while.21 = (s32[]{:T(128)}, f32[4,512,256]{2,1,0:T(8,128)S(1)}, f32[4,3,512]{2,1,0:T(4,128)S(1)}, f32[3,2048]{1,0:T(4,128)S(1)}, f32[2048,256]{1,0:T(8,128)}, /*index=5*/s32[]{:T(128)}, s32[]{:T(128)}, s32[]{}, s32[]{}) while((s32[]{:T(128)}, f32[4,512,256]{2,1,0:T(8,128)S(1)}, f32[4,3,512]{2,1,0:T(4,128)S(1)}, f32[3,2048]{1,0:T(4,128)S(1)}, ...), condition=%wide.region_12.13_spmd, body=%wide.region_11.12_spmd.sunk | while | flops 3231711232 | bytes 2713733 | solution.py:33
  436.9 6.4 %fusion.75 = f32[4,512,256]{2,1,0:T(8,128)S(1)} fusion(f32[4,512,256]{2,1,0:T(8,128)S(1)} %get-tuple-element.219, s32[]{:T(128)} %get-tuple-element.218, f32[2048,256]{1,0:T(8,128)} %get-tuple-element.231, f32[2048]{0:T(1024)S(1)} %bitcast.66, f32[512]{0:T(512)S(1)} %bitcast.73, f32[2048]{0:T(1024)S(1)} %bitcast.67, f32[512]{0:T(512)S(1)} %bitcast.72, ...), kind=kOutput, calls=%fused_computation.48.clone.1 | convolution fusion | flops 3231711232 | bytes 2652164 | tf_op jit(solution)/shard_map/while/body/eval_jaxpr/dot_general | solution.py:29
  443.4 6.4 %fusion.75 = f32[4,512,256]{2,1,0:T(8,128)S(1)} fusion(f32[4,512,256]{2,1,0:T(8,128)S(1)} %get-tuple-element.219, s32[]{:T(128)} %get-tuple-element.218, f32[2048,256]{1,0:T(8,128)} %get-tuple-element.231, f32[2048]{0:T(1024)S(1)} %bitcast.66, f32[512]{0:T(512)S(1)} %bitcast.73, f32[2048]{0:T(1024)S(1)} %bitcast.67, f32[512]{0:T(512)S(1)} %bitcast.72, ...), kind=kOutput, calls=%fused_computation.48.clone.1 | convolution fusion | flops 3231711232 | bytes 2652164 | tf_op jit(solution)/shard_map/while/body/eval_jaxpr/dot_general | solution.py:29
  449.9 6.4 %fusion.75 = f32[4,512,256]{2,1,0:T(8,128)S(1)} fusion(f32[4,512,256]{2,1,0:T(8,128)S(1)} %get-tuple-element.219, s32[]{:T(128)} %get-tuple-element.218, f32[2048,256]{1,0:T(8,128)} %get-tuple-element.231, f32[2048]{0:T(1024)S(1)} %bitcast.66, f32[512]{0:T(512)S(1)} %bitcast.73, f32[2048]{0:T(1024)S(1)} %bitcast.67, f32[512]{0:T(512)S(1)} %bitcast.72, ...), kind=kOutput, calls=%fused_computation.48.clone.1 | convolution fusion | flops 3231711232 | bytes 2652164 | tf_op jit(solution)/shard_map/while/body/eval_jaxpr/dot_general | solution.py:29
  456.3 6.4 %fusion.75 = f32[4,512,256]{2,1,0:T(8,128)S(1)} fusion(f32[4,512,256]{2,1,0:T(8,128)S(1)} %get-tuple-element.219, s32[]{:T(128)} %get-tuple-element.218, f32[2048,256]{1,0:T(8,128)} %get-tuple-element.231, f32[2048]{0:T(1024)S(1)} %bitcast.66, f32[512]{0:T(512)S(1)} %bitcast.73, f32[2048]{0:T(1024)S(1)} %bitcast.67, f32[512]{0:T(512)S(1)} %bitcast.72, ...), kind=kOutput, calls=%fused_computation.48.clone.1 | convolution fusion | flops 3231711232 | bytes 2652164 | tf_op jit(solution)/shard_map/while/body/eval_jaxpr/dot_general | solution.py:29
  462.8 1.3 copy-done
  464.1 61.9 %reduce-scatter.5.cloned.1.call-done = f32[128,256]{1,0:T(8,128)} async-done(((f32[2048,256]{1,0:T(8,128)}), f32[128,256]{1,0:T(8,128)}) %reduce-scatter.5.cloned.1.call-update) | async-done | bytes 131088 | tf_op jit(solution)/shard_map/reduce_scatter | solution.py:59
  527.0 79.5 %psum.47 = f32[256]{0:T(256)S(1)} all-reduce(f32[256]{0:T(256)S(1)} %multiply_reduce_fusion), channel_id=1, replica_groups=mesh['row'=16,'col'=16] {'row','col'}, use_global_device_ids=true, to_apply=%region_15.16 | all-reduce | flops 256 | bytes 2048 | tf_op jit(solution)/shard_map/psum | solution.py:66
  606.5 1.7 multiply_subtract_fusion
  (42 shorter events, 5.4 us)
Async XLA Ops:
  7.2 69.5 %all-gather.3.cloned.1.call-start = ((), (), s32[]{:S(2)}) async-start(), calls=%async_computation.2 | async-start | bytes 2228224 | tf_op jit(solution)/shard_map/all_gather | solution.py:58
  7.9 154.7 %reduce-scatter.3.cloned.1.call-start = ((), (), s32[]{:S(2)}) async-start(), calls=%async_computation.3 | async-start | bytes 2228224 | tf_op jit(solution)/shard_map/reduce_scatter | solution.py:59
  102.7 1.4 copy-start.1
  102.7 59.9 %copy-start.2 = (f32[128,256]{1,0:T(8,128)S(1)}, f32[128,256]{1,0:T(8,128)}, u32[]{:S(2)}) copy-start(f32[128,256]{1,0:T(8,128)} %param.9) | copy-start | bytes 393220
  102.7 59.9 %copy-start.4 = (f32[128]{0:T(128)S(1)}, f32[128]{0:T(128)}, u32[]{:S(2)}) copy-start(f32[128]{0:T(128)} %param.8) | copy-start | bytes 1540
  104.1 332.6 %all-gather.5.cloned.1.call-start = ((), (), s32[]{:S(2)}) async-start(), calls=%async_computation.4 | async-start | bytes 2228224 | tf_op jit(solution)/shard_map/all_gather | solution.py:58
  375.5 150.5 %reduce-scatter.5.cloned.1.call-start = ((), (), s32[]{:S(2)}) async-start(), calls=%async_computation.5 | async-start | bytes 2228224 | tf_op jit(solution)/shard_map/reduce_scatter | solution.py:59
  462.7 1.4 copy-start
  462.8 63.3 %copy-start.3 = (f32[128,256]{1,0:T(8,128)S(1)}, f32[128,256]{1,0:T(8,128)}, u32[]{:S(2)}) copy-start(f32[128,256]{1,0:T(8,128)} %multiply_add_fusion.1) | copy-start | bytes 393220
Sparse Core Ops, SparseCore 0:
  10.4 62.6 all-gather.2
  104.2 58.3 reduce-scatter.2
  375.6 61.0 all-gather.4
  464.2 61.7 reduce-scatter.4
